TPU v7x, 32 devices: a whole 2x2x4 slice. The times are simulated.
32 devices in a mesh: row: 8 (over z, core), feat: 4 (over y, x).
Axes of the slice: x: 2, y: 2, z: 4, core: 2. Of those that a mesh axis runs over, the one named last changes fastest.
Arguments:
- grads: bfloat16 [64, 16384], P(None, ('row', 'feat')), may hold values from -0.75 to 0.75
- codes: int32 [256, 16384], P('feat', 'row'), may hold values from 0 to 127
- node_ids: int32 [16384], P('row'), may hold values from 0 to 7, as said below
- node_slot: int32 [8], replicated, may hold values from 0 to 7, each once
Outputs:
- owned_hist: float32 [8, 64, 32768], P('row', None, 'feat')
Inputs may be any that keep to these rules, and one draw needn't show every extreme that they name: `node_ids`: within each panel of 2048 rows the node ids never fall, every node has at most 512 rows in a panel, and every panel has a node with exactly 512 rows.
All inputs are finite; a program needn't handle non-finite values.
Results may differ from a plain program's by a relative error of at most 0.0028.
Values may be sent and summed in bfloat16 or wider, within the bound.
A program may use at most 64 MiB of HBM per device.

v0:
```python
import jax
import jax.numpy as jnp
from jax import lax
from jax.sharding import PartitionSpec as P

BINS = 128


def window_parts(gathered, codes, node_ids, node_id, row_start, span, align):
    aligned = row_start // align * align
    start = jnp.minimum(aligned, gathered.shape[1] - span)
    grads_window = lax.dynamic_slice_in_dim(gathered, start, span, 1)
    ids_window = lax.dynamic_slice_in_dim(node_ids, start, span, 0)
    codes_window = lax.dynamic_slice_in_dim(codes, start, span, 1)
    masked = jnp.where((ids_window == node_id)[None, :], grads_window, jnp.zeros_like(grads_window))
    return (masked, codes_window)


def bin_table(codes_window):
    levels = jnp.arange(BINS, dtype=jnp.int32)
    table = (codes_window[:, None, :] == levels[None, :, None]).astype(jnp.bfloat16)
    return table.reshape(codes_window.shape[0] * BINS, codes_window.shape[1])


def tile_of(grad_rows, code_rows):
    return lax.dot_general(
        grad_rows,
        bin_table(code_rows),
        (((1,), (1,)), ((), ())),
        preferred_element_type=jnp.float32,
    )


def on_device(grads, codes, node_ids, node_slot):
    gathered = lax.all_gather(grads, "feat", axis=1, tiled=True)
    owners = lax.axis_size("row")
    total_nodes = node_slot.shape[0]
    length = gathered.shape[1]
    capacity = 2 * length // total_nodes
    node_levels = jnp.arange(total_nodes, dtype=jnp.int32)
    row_starts = jnp.sum((node_ids[:, None] < node_levels[None, :]).astype(jnp.int32), axis=0)
    picks = node_slot[:, None] == node_levels[None, :]
    slot_starts = jnp.sum(jnp.where(picks, row_starts[None, :], 0), axis=1)
    align = 128
    span = capacity + align
    groups = total_nodes // 2
    grouped = (node_slot.reshape(groups, 2), slot_starts.reshape(groups, 2))

    def group_tiles(pieces):

        def node_tile(node_id, row_start):
            masked, codes_window = window_parts(
                gathered, codes, node_ids, node_id, row_start, span, align
            )
            return tile_of(masked, codes_window).astype(jnp.bfloat16)

        return jax.vmap(node_tile)(pieces[0], pieces[1])

    tiles = lax.map(group_tiles, grouped)
    tiles = tiles.reshape(total_nodes, tiles.shape[2], tiles.shape[3])
    received = lax.all_to_all(tiles, "row", split_axis=0, concat_axis=0, tiled=True)
    stacked = received.reshape(owners, -1, received.shape[1], received.shape[2])
    return jnp.sum(stacked, axis=0, dtype=jnp.float32)


def solution(mesh):
    in_specs = (P(None, ("row", "feat")), P("feat", "row"), P("row"), P())
    out_specs = P("row", None, "feat")
    return jax.shard_map(
        on_device, mesh=mesh, in_specs=in_specs, out_specs=out_specs, check_vma=False
    )
```

profile of v0, /device:TPU:8, one launch (start us, length us, event | category | flops | bytes accessed | tf_op | source)
XLA Modules:
  0.0 328.3 jit_solution(12369513912950885408)
XLA Ops:
  0.0 9.3 %all_gather.3 = bf16[64,2048]{1,0:T(8,128)(2,1)S(1)} all-gather(bf16[64,512]{1,0:T(8,128)(2,1)} %param.6), channel_id=1, replica_groups=mesh['row'=8,'feat'=4] {'feat'}, dimensions={1}, use_global_device_ids=true | all-gather | bytes 327680 | tf_op jit(solution)/shard_map/all_gather | solution.py:35
  9.3 0.8 convert_reduce_fusion.1
  10.1 0.7 reshape.142
  10.8 0.8 select_reduce_fusion
  11.8 126.8 %while.28 = (s32[]{:T(128)}, bf16[4,2,64,8192]{3,2,1,0:T(8,128)(2,1)}, s32[4,2]{1,0:T(4,128)S(1)}, s32[2048]{0:T(1024)}, s32[4,2]{1,0:T(4,128)S(1)}, /*index=5*/...) while((s32[]{:T(128)}, ...), condition=%wide.region_3.4_spmd.clone, body=%wide.region_2.3_spmd.sunk.clone | while | flops 1353794816 | bytes 24141428 | solution.py:59
  11.8 4.4 %while.27 = (s32[]{:T(128)}, s32[2048]{0:T(1024)}, s32[2,1]{0,1:T(1,128)S(1)}, s32[2,640]{1,0:T(2,128)S(1)}, s32[]{:T(128)}, /*index=5*/s32[]{:T(128)}) while((s32[]{:T(128)}, s32[2048]{0:T(1024)}, s32[2,1]{0,1:T(1,128)S(1)}, s32[2,640]{1,0:T(2,128)S(1)}, s32[]{:T(128)}, /*index=5*/s32[]{:T(128)}) %tuple.89), condition=%wide.while_cond, body=%wide.while_body.sunk | while | flops 2 | bytes 15449 | solution.py:13
  12.5 1.5 dynamic-slice.27
  14.6 1.5 dynamic-slice.27
  16.4 4.8 %while.25 = (s32[]{:T(128)}, s32[64,2048]{1,0:T(8,128)}, s32[2,2]{1,0:T(2,128)S(1)}, s32[2,64,640]{2,1,0:T(8,128)S(1)}, s32[]{:T(128)}) while((s32[]{:T(128)}, s32[64,2048]{1,0:T(8,128)}, s32[2,2]{1,0:T(2,128)S(1)}, s32[2,64,640]{2,1,0:T(8,128)S(1)}, s32[]{:T(128)}) %tuple.83), condition=%wide.while_cond.2, body=%wide.while_body.2.sunk | while | flops 2 | bytes 327777 | solution.py:14
  17.1 1.7 bitcast_dynamic-update-slice_fusion.4
  19.5 1.7 bitcast_dynamic-update-slice_fusion.4
  21.3 7.6 %bitcast_compare_fusion.3 = pred[2,8192,640]{2,1,0:T(32,128)(4,1)} fusion(s32[8192]{0:T(1024)S(1)} %iota_bitcast_fusion.3, s32[2,64,640]{2,1,0:T(8,128)S(1)} %get-tuple-element.341), kind=kLoop, calls=%fused_computation.5.clone.1.clone | loop fusion | flops 10485760 | bytes 10846208 | tf_op jit(solution)/shard_map/while/body/eval_jaxpr/vmap()/eq | solution.py:21
  28.9 2.7 while.26
  31.5 11.9 %fusion.20 = bf16[4,2,64,8192]{3,2,1,0:T(8,128)(2,1)} fusion(bf16[4,2,64,8192]{3,2,1,0:T(8,128)(2,1)} %get-tuple-element.422, s32[]{:T(128)} %get-tuple-element.421, pred[2,8192,640]{2,1,0:T(32,128)(4,1)} %bitcast_compare_fusion.3, bf16[2,64,640]{2,1,0:T(8,128)(2,1)S(1)} %get-tuple-element.342, pred[2,640]{1,0:T(4,128)(4,1)S(1)} %broadcast_compare_fusion.3), kind=kOutput, calls=%fused_computation.8.clone.1.clone | convolution fusion | flops 1343307776 | bytes 12748544 | tf_op jit(solution)/shard_map/while/body/eval_jaxpr/vmap()/dot_general | solution.py:26
  43.4 4.4 %while.27 = (s32[]{:T(128)}, s32[2048]{0:T(1024)}, s32[2,1]{0,1:T(1,128)S(1)}, s32[2,640]{1,0:T(2,128)S(1)}, s32[]{:T(128)}, /*index=5*/s32[]{:T(128)}) while((s32[]{:T(128)}, s32[2048]{0:T(1024)}, s32[2,1]{0,1:T(1,128)S(1)}, s32[2,640]{1,0:T(2,128)S(1)}, s32[]{:T(128)}, /*index=5*/s32[]{:T(128)}) %tuple.89), condition=%wide.while_cond, body=%wide.while_body.sunk | while | flops 2 | bytes 15449 | solution.py:13
  44.1 1.5 dynamic-slice.27
  46.3 1.5 dynamic-slice.27
  48.1 4.8 %while.25 = (s32[]{:T(128)}, s32[64,2048]{1,0:T(8,128)}, s32[2,2]{1,0:T(2,128)S(1)}, s32[2,64,640]{2,1,0:T(8,128)S(1)}, s32[]{:T(128)}) while((s32[]{:T(128)}, s32[64,2048]{1,0:T(8,128)}, s32[2,2]{1,0:T(2,128)S(1)}, s32[2,64,640]{2,1,0:T(8,128)S(1)}, s32[]{:T(128)}) %tuple.83), condition=%wide.while_cond.2, body=%wide.while_body.2.sunk | while | flops 2 | bytes 327777 | solution.py:14
  48.7 1.7 bitcast_dynamic-update-slice_fusion.4
  51.2 1.7 bitcast_dynamic-update-slice_fusion.4
  52.9 7.6 %bitcast_compare_fusion.3 = pred[2,8192,640]{2,1,0:T(32,128)(4,1)} fusion(s32[8192]{0:T(1024)S(1)} %iota_bitcast_fusion.3, s32[2,64,640]{2,1,0:T(8,128)S(1)} %get-tuple-element.341), kind=kLoop, calls=%fused_computation.5.clone.1.clone | loop fusion | flops 10485760 | bytes 10846208 | tf_op jit(solution)/shard_map/while/body/eval_jaxpr/vmap()/eq | solution.py:21
  60.5 2.7 while.26
  62.4 0.7 bitcast_dynamic-update-slice_fusion.5
  63.2 12.0 %fusion.20 = bf16[4,2,64,8192]{3,2,1,0:T(8,128)(2,1)} fusion(bf16[4,2,64,8192]{3,2,1,0:T(8,128)(2,1)} %get-tuple-element.422, s32[]{:T(128)} %get-tuple-element.421, pred[2,8192,640]{2,1,0:T(32,128)(4,1)} %bitcast_compare_fusion.3, bf16[2,64,640]{2,1,0:T(8,128)(2,1)S(1)} %get-tuple-element.342, pred[2,640]{1,0:T(4,128)(4,1)S(1)} %broadcast_compare_fusion.3), kind=kOutput, calls=%fused_computation.8.clone.1.clone | convolution fusion | flops 1343307776 | bytes 12748544 | tf_op jit(solution)/shard_map/while/body/eval_jaxpr/vmap()/dot_general | solution.py:26
  75.2 4.4 %while.27 = (s32[]{:T(128)}, s32[2048]{0:T(1024)}, s32[2,1]{0,1:T(1,128)S(1)}, s32[2,640]{1,0:T(2,128)S(1)}, s32[]{:T(128)}, /*index=5*/s32[]{:T(128)}) while((s32[]{:T(128)}, s32[2048]{0:T(1024)}, s32[2,1]{0,1:T(1,128)S(1)}, s32[2,640]{1,0:T(2,128)S(1)}, s32[]{:T(128)}, /*index=5*/s32[]{:T(128)}) %tuple.89), condition=%wide.while_cond, body=%wide.while_body.sunk | while | flops 2 | bytes 15449 | solution.py:13
  75.8 1.5 dynamic-slice.27
  78.0 1.5 dynamic-slice.27
  79.8 4.8 %while.25 = (s32[]{:T(128)}, s32[64,2048]{1,0:T(8,128)}, s32[2,2]{1,0:T(2,128)S(1)}, s32[2,64,640]{2,1,0:T(8,128)S(1)}, s32[]{:T(128)}) while((s32[]{:T(128)}, s32[64,2048]{1,0:T(8,128)}, s32[2,2]{1,0:T(2,128)S(1)}, s32[2,64,640]{2,1,0:T(8,128)S(1)}, s32[]{:T(128)}) %tuple.83), condition=%wide.while_cond.2, body=%wide.while_body.2.sunk | while | flops 2 | bytes 327777 | solution.py:14
  80.5 1.7 bitcast_dynamic-update-slice_fusion.4
  82.9 1.7 bitcast_dynamic-update-slice_fusion.4
  84.6 7.6 %bitcast_compare_fusion.3 = pred[2,8192,640]{2,1,0:T(32,128)(4,1)} fusion(s32[8192]{0:T(1024)S(1)} %iota_bitcast_fusion.3, s32[2,64,640]{2,1,0:T(8,128)S(1)} %get-tuple-element.341), kind=kLoop, calls=%fused_computation.5.clone.1.clone | loop fusion | flops 10485760 | bytes 10846208 | tf_op jit(solution)/shard_map/while/body/eval_jaxpr/vmap()/eq | solution.py:21
  92.2 2.7 while.26
  92.8 0.7 bitcast_dynamic-update-slice_fusion.5
  94.2 0.7 bitcast_dynamic-update-slice_fusion.5
  94.9 11.9 %fusion.20 = bf16[4,2,64,8192]{3,2,1,0:T(8,128)(2,1)} fusion(bf16[4,2,64,8192]{3,2,1,0:T(8,128)(2,1)} %get-tuple-element.422, s32[]{:T(128)} %get-tuple-element.421, pred[2,8192,640]{2,1,0:T(32,128)(4,1)} %bitcast_compare_fusion.3, bf16[2,64,640]{2,1,0:T(8,128)(2,1)S(1)} %get-tuple-element.342, pred[2,640]{1,0:T(4,128)(4,1)S(1)} %broadcast_compare_fusion.3), kind=kOutput, calls=%fused_computation.8.clone.1.clone | convolution fusion | flops 1343307776 | bytes 12748544 | tf_op jit(solution)/shard_map/while/body/eval_jaxpr/vmap()/dot_general | solution.py:26
  106.8 4.4 %while.27 = (s32[]{:T(128)}, s32[2048]{0:T(1024)}, s32[2,1]{0,1:T(1,128)S(1)}, s32[2,640]{1,0:T(2,128)S(1)}, s32[]{:T(128)}, /*index=5*/s32[]{:T(128)}) while((s32[]{:T(128)}, s32[2048]{0:T(1024)}, s32[2,1]{0,1:T(1,128)S(1)}, s32[2,640]{1,0:T(2,128)S(1)}, s32[]{:T(128)}, /*index=5*/s32[]{:T(128)}) %tuple.89), condition=%wide.while_cond, body=%wide.while_body.sunk | while | flops 2 | bytes 15449 | solution.py:13
  107.5 1.5 dynamic-slice.27
  109.7 1.5 dynamic-slice.27
  111.5 4.8 %while.25 = (s32[]{:T(128)}, s32[64,2048]{1,0:T(8,128)}, s32[2,2]{1,0:T(2,128)S(1)}, s32[2,64,640]{2,1,0:T(8,128)S(1)}, s32[]{:T(128)}) while((s32[]{:T(128)}, s32[64,2048]{1,0:T(8,128)}, s32[2,2]{1,0:T(2,128)S(1)}, s32[2,64,640]{2,1,0:T(8,128)S(1)}, s32[]{:T(128)}) %tuple.83), condition=%wide.while_cond.2, body=%wide.while_body.2.sunk | while | flops 2 | bytes 327777 | solution.py:14
  112.1 1.7 bitcast_dynamic-update-slice_fusion.4
  114.6 1.7 bitcast_dynamic-update-slice_fusion.4
  116.3 7.6 %bitcast_compare_fusion.3 = pred[2,8192,640]{2,1,0:T(32,128)(4,1)} fusion(s32[8192]{0:T(1024)S(1)} %iota_bitcast_fusion.3, s32[2,64,640]{2,1,0:T(8,128)S(1)} %get-tuple-element.341), kind=kLoop, calls=%fused_computation.5.clone.1.clone | loop fusion | flops 10485760 | bytes 10846208 | tf_op jit(solution)/shard_map/while/body/eval_jaxpr/vmap()/eq | solution.py:21
  123.9 2.7 while.26
  124.5 0.7 bitcast_dynamic-update-slice_fusion.5
  125.9 0.7 bitcast_dynamic-update-slice_fusion.5
  126.6 12.0 %fusion.20 = bf16[4,2,64,8192]{3,2,1,0:T(8,128)(2,1)} fusion(bf16[4,2,64,8192]{3,2,1,0:T(8,128)(2,1)} %get-tuple-element.422, s32[]{:T(128)} %get-tuple-element.421, pred[2,8192,640]{2,1,0:T(32,128)(4,1)} %bitcast_compare_fusion.3, bf16[2,64,640]{2,1,0:T(8,128)(2,1)S(1)} %get-tuple-element.342, pred[2,640]{1,0:T(4,128)(4,1)S(1)} %broadcast_compare_fusion.3), kind=kOutput, calls=%fused_computation.8.clone.1.clone | convolution fusion | flops 1343307776 | bytes 12748544 | tf_op jit(solution)/shard_map/while/body/eval_jaxpr/vmap()/dot_general | solution.py:26
  138.5 187.0 %all_to_all.5 = bf16[8,64,8192]{2,1,0:T(8,128)(2,1)S(1)} all-to-all(bf16[8,64,8192]{2,1,0:T(8,128)(2,1)} %bitcast.54), channel_id=1, replica_groups=mesh['row'=8,'feat'=4] {'row'}, dimensions={0} | all-to-all | bytes 16777216 | tf_op jit(solution)/shard_map/all_to_all | solution.py:61
  325.6 2.8 convert_reduce_fusion
  (97 shorter events, 19.1 us)
where the time goes:
time: 333 us; the launch traced here: 328 us
  blocking collectives  196 us (59%)
  local copies, waits for them, and re-layouts  48.5 us (15%)
  matrix products  47.7 us (14%)
  other arithmetic  35.2 us (11%)
    all_to_all x1, blocking collectives, on_device(): lax.all_to_all(tiles, 'row', split_axis=0, concat_axis=0, tiled=True)  187 us
    dot_general x4, matrix products, tile_of(): lax.dot_general(grad_rows, bin_table(code_rows), (((1,), (1,)), ((), ()))...  47.7 us
    gather x80, local copies, waits for them, and re-layouts  46.9 us
    eq x4, other arithmetic, bin_table(): codes_window[:, None, :] == levels[None, :, None]  30.4 us
    all_gather x1, blocking collectives, on_device(): gathered = lax.all_gather(grads, 'feat', axis=1, tiled=True)  9.26 us

commit v1 on v0

v1 whole, which is shorter than its diff:
```python
import functools

import jax
import jax.numpy as jnp
from jax import lax
from jax.experimental import pallas as pl
from jax.experimental.pallas import tpu as pltpu
from jax.sharding import PartitionSpec as P

BINS = 128
LANES = 128
OUTSIDE = 255.0
GROUP = 4
CHUNK = 20


def pack_kernel(starts, nodes, ids_ref, codes_ref, grads_ref, out_ref):
    slots, _, span = out_ref.shape
    features = codes_ref.shape[0]
    for j in range(slots):
        start = pl.multiple_of(starts[j], LANES)
        window = pl.ds(start, span)
        inside = ids_ref[:, window] == nodes[j]
        codes = codes_ref[:, window].astype(jnp.float32)
        codes = jnp.where(jnp.broadcast_to(inside, codes.shape), codes, OUTSIDE)
        out_ref[j, :features, :] = codes.astype(jnp.bfloat16)
        out_ref[j, features:, :] = grads_ref[:, window]


def pack_windows(starts, nodes, ids, codes, grads, span):
    slots = starts.shape[0]
    rows = codes.shape[0] + grads.shape[0]
    whole = lambda shape: pl.BlockSpec(shape, lambda *_: (0,) * len(shape))
    return pl.pallas_call(
        pack_kernel,
        out_shape=jax.ShapeDtypeStruct((slots, rows, span), jnp.bfloat16),
        grid_spec=pltpu.PrefetchScalarGridSpec(
            num_scalar_prefetch=2,
            grid=(1,),
            in_specs=[whole(ids.shape), whole(codes.shape), whole(grads.shape)],
            out_specs=whole((slots, rows, span)),
        ),
        compiler_params=pltpu.CompilerParams(vmem_limit_bytes=48 << 20),
        name="pack_windows",
    )(starts, nodes, ids, codes, grads)


def hist_kernel(order, total, recv_ref, out_ref, codes_ref, grads_ref):
    features = out_ref.shape[1] // BINS
    outputs = out_ref.shape[0]
    per_panel = recv_ref.shape[2] // LANES
    most = grads_ref.shape[0] // (2 * LANES)

    def gather(i, _):
        block = order[i]
        panel = block // per_panel
        at = pl.multiple_of((block % per_panel) * LANES, LANES)
        to = pl.multiple_of(i * LANES, LANES)
        codes_ref[:, pl.ds(to, LANES)] = recv_ref[panel, :features, pl.ds(at, LANES)].astype(jnp.float32)
        tile = recv_ref[panel, features:, pl.ds(at, LANES)].astype(jnp.float32)
        grads_ref[pl.ds(to, LANES), :] = tile.T.astype(jnp.bfloat16)
        return 0

    count = total[0]
    lax.fori_loop(0, count, gather, 0)
    steps = (count + 1) // 2

    @pl.when(count % 2 == 1)
    def _():
        to = pl.multiple_of(count * LANES, LANES)
        codes_ref[:, pl.ds(to, LANES)] = jnp.full((features, LANES), OUTSIDE, jnp.float32)
        grads_ref[pl.ds(to, LANES), :] = jnp.zeros((LANES, outputs), jnp.bfloat16)

    @pl.when(count == 0)
    def _():
        out_ref[...] = jnp.zeros_like(out_ref)

    def body(depth, first, add):
        base = lax.broadcasted_iota(jnp.int32, (16, depth), 0).astype(jnp.float32)

        def one(g, _):
            parts = []
            for q in range(GROUP):
                row = codes_ref[pl.ds(g * GROUP + q, 1), pl.ds(first, depth)]
                rows = (jnp.broadcast_to(row, (16, depth)) - base).astype(jnp.bfloat16)
                for b in range(BINS // 16):
                    parts.append(jnp.where(rows == jnp.bfloat16(16 * b), jnp.bfloat16(1), jnp.bfloat16(0)))
            table = jnp.concatenate(parts, axis=0)
            tile = jnp.dot(table, grads_ref[pl.ds(first, depth), :], preferred_element_type=jnp.float32).T
            at = pl.ds(pl.multiple_of(g * GROUP * BINS, GROUP * BINS), GROUP * BINS)
            out_ref[:, at] = out_ref[:, at] + tile if add else tile
            return 0

        lax.fori_loop(0, features // GROUP, one, 0)

    if most <= CHUNK:
        for n in range(1, most + 1):
            pl.when(steps == n)(functools.partial(body, n * 2 * LANES, 0, False))
        return

    out_ref[...] = jnp.zeros_like(out_ref)

    def chunk(c, _):
        first = pl.multiple_of(c * CHUNK * 2 * LANES, LANES)
        here = jnp.minimum(steps - c * CHUNK, CHUNK)
        for n in range(1, CHUNK + 1):
            pl.when(here == n)(functools.partial(body, n * 2 * LANES, first, True))
        return 0

    lax.fori_loop(0, (steps + CHUNK - 1) // CHUNK, chunk, 0)


def node_histogram(order, total, recv, features, outputs):
    panels, rows, span = recv.shape
    blocks = panels * (span // LANES)
    depth = (blocks + 1) // 2 * 2 * LANES
    return pl.pallas_call(
        hist_kernel,
        out_shape=jax.ShapeDtypeStruct((outputs, features * BINS), jnp.float32),
        grid_spec=pltpu.PrefetchScalarGridSpec(
            num_scalar_prefetch=2,
            grid=(1,),
            in_specs=[pl.BlockSpec((panels, rows, span), lambda *_: (0, 0, 0))],
            out_specs=pl.BlockSpec((outputs, features * BINS), lambda *_: (0, 0)),
            scratch_shapes=[
                pltpu.VMEM((features, depth), jnp.float32),
                pltpu.VMEM((depth, outputs), jnp.bfloat16),
            ],
        ),
        compiler_params=pltpu.CompilerParams(vmem_limit_bytes=56 << 20),
        name="node_histogram",
    )(order, total, recv)


def on_device(grads, codes, node_ids, node_slot):
    gathered = lax.all_gather(grads, "feat", axis=1, tiled=True)
    total_nodes = node_slot.shape[0]
    features, length = codes.shape
    outputs = grads.shape[0]
    capacity = 2 * length // total_nodes
    span = capacity + LANES
    row_starts = jnp.sum((node_ids[None, :] < node_slot[:, None]).astype(jnp.int32), axis=1)
    starts = jnp.minimum(row_starts // LANES * LANES, length - span)
    sent = pack_windows(starts, node_slot, node_ids.reshape(1, length), codes, gathered, span)
    recv = lax.all_to_all(sent, "row", split_axis=0, concat_axis=0, tiled=True)
    blocks = recv.shape[0] * (span // LANES)
    filled = (recv[:, 0, :] < BINS).reshape(blocks, LANES).any(axis=1)
    index = jnp.arange(blocks, dtype=jnp.int32)
    rank = jnp.sum((filled[None, :] & (index[None, :] < index[:, None])).astype(jnp.int32), axis=1)
    hit = filled[None, :] & (rank[None, :] == index[:, None])
    order = jnp.sum(jnp.where(hit, index[None, :], 0), axis=1)
    total = jnp.sum(filled.astype(jnp.int32)).reshape(1)
    return node_histogram(order, total, recv, features, outputs)[None]


def solution(mesh):
    in_specs = (P(None, ("row", "feat")), P("feat", "row"), P("row"), P())
    out_specs = P("row", None, "feat")
    return jax.shard_map(
        on_device, mesh=mesh, in_specs=in_specs, out_specs=out_specs, check_vma=False
    )
```

time: 333 us -> 77 us (0.23)
  the two profiles are of different devices: /device:TPU:8 before, /device:TPU:0 now
where the time goes in v1:
time: 77 us; the launch traced here: 77.8 us
  blocking collectives  47.6 us (62%)
  Pallas kernels  25.1 us (33%)
  other arithmetic  2.64 us (3%)
  local copies, waits for them, and re-layouts  2.43 us (3%)
    all_to_all x1, blocking collectives, on_device(): recv = lax.all_to_all(sent, 'row', split_axis=0, concat_axis=0, tiled=True)  36.9 us
    pallas_call x1, Pallas kernels, node_histogram(): pl.pallas_call(hist_kernel, out_shape=jax.ShapeDtypeStruct((outputs, feat...  24.4 us
    all_gather x1, blocking collectives, on_device(): gathered = lax.all_gather(grads, 'feat', axis=1, tiled=True)  10.7 us
    unnamed x8, local copies, waits for them, and re-layouts  2.4 us

profile of v1, /device:TPU:0, one launch (start us, length us, event | category | flops | bytes accessed | tf_op | source)
XLA Modules:
  0.0 77.8 jit_solution(11706642568932153984)
XLA Ops:
  0.0 0.9 %convert_reduce_fusion = s32[8]{0:T(128)S(1)} fusion(s32[2048]{0:T(1024)} %param.6, s32[8]{0:T(128)} %nodes.1), kind=kLoop, calls=%fused_computation.1 | loop fusion | flops 49144 | bytes 8256 | tf_op jit(solution)/shard_map/reduce_sum | solution.py:142
  0.9 10.7 %all_gather.3.grads_ref = bf16[64,2048]{1,0:T(8,128)(2,1)S(1)} all-gather(bf16[64,512]{1,0:T(8,128)(2,1)} %param.4), channel_id=1, replica_groups=mesh['row'=8,'feat'=4] {'feat'}, dimensions={1}, use_global_device_ids=true | all-gather | bytes 327680 | tf_op jit(solution)/shard_map/all_gather | solution.py:136
  11.6 0.0 copy-start
  11.6 1.0 %copy-done = s32[64,2048]{1,0:T(8,128)S(1)} copy-done((s32[64,2048]{1,0:T(8,128)S(1)}, s32[64,2048]{1,0:T(8,128)}, u32[]{:S(2)}) %copy-start) | copy-done | bytes 524312
  12.7 0.0 copy-start.1
  12.7 0.7 copy-done.1
  13.4 0.0 copy-start.2
  13.4 0.7 copy-done.2
  14.0 0.7 pack_windows.1
  14.7 36.9 %all_to_all.5.recv_ref = bf16[8,128,640]{2,1,0:T(8,128)(2,1)S(1)} all-to-all(bf16[8,128,640]{2,1,0:T(8,128)(2,1)S(1)} %pack_windows.1), channel_id=1, replica_groups=mesh['row'=8,'feat'=4] {'row'}, dimensions={0} | all-to-all | bytes 2621440 | tf_op jit(solution)/shard_map/all_to_all | solution.py:145
  51.6 0.0 copy-start.3
  51.6 0.1 compare_reduce_fusion
  51.7 0.1 reduce_or.9
  51.8 0.8 convert_reduce_fusion.2
  52.6 0.1 convert_reduce_fusion.1
  52.7 0.7 select_reduce_fusion.order
  53.4 0.0 copy-done.3
  53.4 24.4 %node_histogram.1 = f32[64,8192]{1,0:T(8,128)} custom-call(s32[40]{0:T(128)} %select_reduce_fusion.order, s32[1]{0:T(128)} %bitcast.1.total, bf16[8,128,640]{2,1,0:T(8,128)(2,1)} %copy-done.3), custom_call_target="tpu_custom_call" | custom-call | tf_op jit(solution)/shard_map/node_histogram/pallas_call | solution.py:117
  (2 shorter events, 0.0 us)
Async XLA Ops:
  11.6 1.0 %copy-start = (s32[64,2048]{1,0:T(8,128)S(1)}, s32[64,2048]{1,0:T(8,128)}, u32[]{:S(2)}) copy-start(s32[64,2048]{1,0:T(8,128)} %codes_ref.1) | copy-start | bytes 1572868
  12.7 0.7 copy-start.1
  13.4 0.7 copy-start.2
  51.6 1.8 %copy-start.3 = (bf16[8,128,640]{2,1,0:T(8,128)(2,1)}, bf16[8,128,640]{2,1,0:T(8,128)(2,1)S(1)}, u32[]{:S(2)}) copy-start(bf16[8,128,640]{2,1,0:T(8,128)(2,1)S(1)} %all_to_all.5.recv_ref) | copy-start | bytes 3932164

commit v2 on v1

v2 whole, which is shorter than its diff:
```python
import functools

import jax
import jax.numpy as jnp
from jax import lax
from jax.experimental import pallas as pl
from jax.experimental.pallas import tpu as pltpu
from jax.sharding import PartitionSpec as P

BINS = 128
LANES = 128
OUTSIDE = 255
MESH = pl.DeviceIdType.MESH
GROUP = 4
CHUNK = 16


def around(count, start, body):
    lax.fori_loop(1, count, lambda d, _: (body(lax.rem(start + d, count)), 0)[1], 0)


def regroup_kernel(grads_ref, out_ref, send, recv, own_sem):
    groups, _, piece = grads_ref.shape
    row, feat = lax.axis_index("row"), lax.axis_index("feat")

    def part(owner):
        return out_ref.at[:, pl.ds(pl.multiple_of(owner * piece, LANES), piece)]

    def copy(peer, owner):
        return pltpu.make_async_remote_copy(
            grads_ref.at[peer], part(owner), send.at[peer], recv.at[owner], (row, peer), MESH
        )

    barrier = pltpu.get_barrier_semaphore()
    around(groups, feat, lambda f: pl.semaphore_signal(barrier, 1, device_id=(row, f), device_id_type=MESH))
    own = pltpu.make_async_copy(grads_ref.at[feat], part(feat), own_sem)
    own.start()
    pl.semaphore_wait(barrier, groups - 1)
    around(groups, feat, lambda f: copy(f, feat).start())
    own.wait()
    around(groups, feat, lambda f: copy(feat, f).wait_recv())
    around(groups, feat, lambda f: copy(f, feat).wait_send())


def regroup(grads):
    groups = lax.axis_size("feat")
    outputs, piece = grads.shape
    share = outputs // groups
    vectors = pl.BlockSpec(memory_space=pltpu.VMEM)
    return pl.pallas_call(
        regroup_kernel,
        out_shape=jax.ShapeDtypeStruct((share, groups * piece), jnp.bfloat16),
        in_specs=[vectors],
        out_specs=vectors,
        scratch_shapes=[
            pltpu.SemaphoreType.DMA((groups,)),
            pltpu.SemaphoreType.DMA((groups,)),
            pltpu.SemaphoreType.DMA,
        ],
        compiler_params=pltpu.CompilerParams(collective_id=0, has_side_effects=True),
        name="regroup",
    )(grads.reshape(groups, share, piece))


def pack_kernel(starts, offsets, nodes, ids_ref, codes_ref, grads_ref, codes_out, grads_out):
    slots, _, capacity = codes_out.shape
    span = capacity + LANES
    for j in range(slots):
        window = pl.ds(pl.multiple_of(starts[j], LANES), span)
        inside = ids_ref[:, window] == nodes[j]
        part = codes_ref[:, window]
        part = jnp.where(jnp.broadcast_to(inside, part.shape), part, OUTSIDE)
        codes_out[j] = pltpu.roll(part, offsets[j], 1)[:, :capacity].astype(jnp.float32).astype(jnp.bfloat16)
        part = grads_ref[:, window].astype(jnp.float32)
        grads_out[j] = pltpu.roll(part, offsets[j], 1)[:, :capacity].astype(jnp.bfloat16)


def pack_windows(starts, offsets, nodes, ids, codes, grads, capacity):
    slots = starts.shape[0]
    scalars = pl.BlockSpec(memory_space=pltpu.SMEM)
    vectors = pl.BlockSpec(memory_space=pltpu.VMEM)
    return pl.pallas_call(
        pack_kernel,
        out_shape=(
            jax.ShapeDtypeStruct((slots, codes.shape[0], capacity), jnp.bfloat16),
            jax.ShapeDtypeStruct((slots, grads.shape[0], capacity), jnp.bfloat16),
        ),
        in_specs=[scalars] * 3 + [vectors] * 3,
        out_specs=(vectors, vectors),
        compiler_params=pltpu.CompilerParams(vmem_limit_bytes=40 << 20),
        name="pack_windows",
    )(starts, offsets, nodes, ids, codes, grads)


def exchange_kernel(
    codes_sent, grads_sent, codes_out, grads_out, code_send, code_recv,
    grad_send, grad_recv, spread_send, spread_recv, own_sem,
):
    owners, groups = grads_out.shape[:2]
    row, feat = lax.axis_index("row"), lax.axis_index("feat")

    def code_copy(peer, owner):
        return pltpu.make_async_remote_copy(
            codes_sent.at[peer], codes_out.at[owner],
            code_send.at[peer], code_recv.at[owner], (peer, feat), MESH,
        )

    def grad_copy(peer, owner):
        return pltpu.make_async_remote_copy(
            grads_sent.at[peer], grads_out.at[owner, feat],
            grad_send.at[peer], grad_recv.at[owner], (peer, feat), MESH,
        )

    def spread_copy(panel, peer, owner):
        return pltpu.make_async_remote_copy(
            grads_out.at[panel, owner], grads_out.at[panel, owner],
            spread_send.at[panel, peer], spread_recv.at[panel, owner], (row, peer), MESH,
        )

    def every_panel(body):
        lax.fori_loop(0, owners, lambda p, _: (around(groups, feat, lambda f: body(p, f)), 0)[1], 0)

    barrier = pltpu.get_barrier_semaphore()
    around(groups, feat, lambda f: pl.semaphore_signal(barrier, 1, device_id=(row, f), device_id_type=MESH))
    around(owners, row, lambda r: pl.semaphore_signal(barrier, 1, device_id=(r, feat), device_id_type=MESH))
    own_grads = pltpu.make_async_copy(grads_sent.at[row], grads_out.at[row, feat], own_sem.at[0])
    own_codes = pltpu.make_async_copy(codes_sent.at[row], codes_out.at[row], own_sem.at[1])
    own_grads.start()
    own_codes.start()
    pl.semaphore_wait(barrier, owners + groups - 2)
    around(owners, row, lambda r: grad_copy(r, row).start())
    around(owners, row, lambda r: code_copy(r, row).start())
    own_grads.wait()
    around(groups, feat, lambda f: spread_copy(row, f, feat).start())

    def spread(panel):
        grad_copy(row, panel).wait_recv()
        around(groups, feat, lambda f: spread_copy(panel, f, feat).start())

    around(owners, row, spread)
    own_codes.wait()
    around(owners, row, lambda r: code_copy(row, r).wait_recv())
    every_panel(lambda p, f: spread_copy(p, feat, f).wait_recv())
    around(owners, row, lambda r: code_copy(r, row).wait_send())
    around(owners, row, lambda r: grad_copy(r, row).wait_send())
    every_panel(lambda p, f: spread_copy(p, f, feat).wait_send())


def exchange(codes, grads):
    groups = lax.axis_size("feat")
    owners, _, capacity = codes.shape
    vectors = pl.BlockSpec(memory_space=pltpu.VMEM)
    return pl.pallas_call(
        exchange_kernel,
        out_shape=(
            jax.ShapeDtypeStruct(codes.shape, jnp.bfloat16),
            jax.ShapeDtypeStruct((owners, groups, grads.shape[1], capacity), jnp.bfloat16),
        ),
        in_specs=[vectors] * 2,
        out_specs=(vectors, vectors),
        scratch_shapes=[pltpu.SemaphoreType.DMA((owners,))] * 4
        + [pltpu.SemaphoreType.DMA((owners, groups))] * 2
        + [pltpu.SemaphoreType.DMA((2,))],
        compiler_params=pltpu.CompilerParams(
            collective_id=1, has_side_effects=True, vmem_limit_bytes=40 << 20
        ),
        name="exchange",
    )(codes, grads)


def hist_kernel(order, total, codes_in, grads_in, out_ref, codes_ref, grads_ref):
    features = out_ref.shape[1] // BINS
    outputs = out_ref.shape[0]
    per_panel = codes_in.shape[2] // LANES
    most = grads_ref.shape[0] // (2 * LANES)

    def gather(i, _):
        block = order[i]
        panel = block // per_panel
        at = pl.multiple_of((block % per_panel) * LANES, LANES)
        to = pl.multiple_of(i * LANES, LANES)
        codes_ref[:, pl.ds(to, LANES)] = codes_in[panel, :, pl.ds(at, LANES)].astype(jnp.float32)
        tile = grads_in[panel, :, pl.ds(at, LANES)].astype(jnp.float32)
        grads_ref[pl.ds(to, LANES), :] = tile.T.astype(jnp.bfloat16)
        return 0

    count = total[0]
    lax.fori_loop(0, count, gather, 0)
    steps = (count + 1) // 2

    @pl.when(count % 2 == 1)
    def _():
        to = pl.multiple_of(count * LANES, LANES)
        codes_ref[:, pl.ds(to, LANES)] = jnp.full((features, LANES), OUTSIDE, jnp.float32)
        grads_ref[pl.ds(to, LANES), :] = jnp.zeros((LANES, outputs), jnp.bfloat16)

    @pl.when(count == 0)
    def _():
        out_ref[...] = jnp.zeros_like(out_ref)

    def body(depth, first, add):
        base = lax.broadcasted_iota(jnp.int32, (16, depth), 0).astype(jnp.float32)

        def one(g, _):
            parts = []
            for q in range(GROUP):
                row = codes_ref[pl.ds(g * GROUP + q, 1), pl.ds(first, depth)]
                rows = (jnp.broadcast_to(row, (16, depth)) - base).astype(jnp.bfloat16)
                for b in range(BINS // 16):
                    parts.append(jnp.where(rows == jnp.bfloat16(16 * b), jnp.bfloat16(1), jnp.bfloat16(0)))
            table = jnp.concatenate(parts, axis=0)
            tile = jnp.dot(table, grads_ref[pl.ds(first, depth), :], preferred_element_type=jnp.float32).T
            at = pl.ds(pl.multiple_of(g * GROUP * BINS, GROUP * BINS), GROUP * BINS)
            out_ref[:, at] = out_ref[:, at] + tile if add else tile
            return 0

        lax.fori_loop(0, features // GROUP, one, 0)

    if most <= CHUNK:
        for n in range(1, most + 1):
            pl.when(steps == n)(functools.partial(body, n * 2 * LANES, 0, False))
        return

    out_ref[...] = jnp.zeros_like(out_ref)

    def chunk(c, _):
        first = pl.multiple_of(c * CHUNK * 2 * LANES, LANES)
        here = jnp.minimum(steps - c * CHUNK, CHUNK)
        for n in range(1, CHUNK + 1):
            pl.when(here == n)(functools.partial(body, n * 2 * LANES, first, True))
        return 0

    lax.fori_loop(0, (steps + CHUNK - 1) // CHUNK, chunk, 0)


def node_histogram(order, total, codes, grads):
    panels, features, capacity = codes.shape
    outputs = grads.shape[1]
    blocks = panels * (capacity // LANES)
    depth = (blocks + 1) // 2 * 2 * LANES
    return pl.pallas_call(
        hist_kernel,
        out_shape=jax.ShapeDtypeStruct((outputs, features * BINS), jnp.float32),
        grid_spec=pltpu.PrefetchScalarGridSpec(
            num_scalar_prefetch=2,
            grid=(1,),
            in_specs=[
                pl.BlockSpec(codes.shape, lambda *_: (0, 0, 0)),
                pl.BlockSpec(grads.shape, lambda *_: (0, 0, 0)),
            ],
            out_specs=pl.BlockSpec((outputs, features * BINS), lambda *_: (0, 0)),
            scratch_shapes=[
                pltpu.VMEM((features, depth), jnp.float32),
                pltpu.VMEM((depth, outputs), jnp.bfloat16),
            ],
        ),
        compiler_params=pltpu.CompilerParams(vmem_limit_bytes=56 << 20),
        name="node_histogram",
    )(order, total, codes, grads)


def on_device(grads, codes, node_ids, node_slot):
    total_nodes = node_slot.shape[0]
    length = codes.shape[1]
    capacity = 2 * length // total_nodes
    span = capacity + LANES
    row_starts = jnp.sum((node_ids[None, :] < node_slot[:, None]).astype(jnp.int32), axis=1)
    starts = jnp.minimum(row_starts // LANES * LANES, length - span)
    offsets = (span - (row_starts - starts)) % span
    panel = regroup(grads)
    sent = pack_windows(
        starts, offsets, node_slot, node_ids.reshape(1, length), codes, panel, capacity
    )
    codes_in, grads_in = exchange(*sent)
    grads_in = grads_in.reshape(grads_in.shape[0], -1, capacity)
    blocks = codes_in.shape[0] * (capacity // LANES)
    filled = (codes_in[:, 0, :] < BINS).reshape(blocks, LANES).any(axis=1)
    index = jnp.arange(blocks, dtype=jnp.int32)
    rank = jnp.sum((filled[None, :] & (index[None, :] < index[:, None])).astype(jnp.int32), axis=1)
    hit = filled[None, :] & (rank[None, :] == index[:, None])
    order = jnp.sum(jnp.where(hit, index[None, :], 0), axis=1)
    total = jnp.sum(filled.astype(jnp.int32)).reshape(1)
    return node_histogram(order, total, codes_in, grads_in)[None]


def solution(mesh):
    in_specs = (P(None, ("row", "feat")), P("feat", "row"), P("row"), P())
    out_specs = P("row", None, "feat")
    return jax.shard_map(
        on_device, mesh=mesh, in_specs=in_specs, out_specs=out_specs, check_vma=False
    )
```

time: 77 us -> 57.3 us (0.74)
  the two profiles are of different devices: /device:TPU:0 before, /device:TPU:8 now
where the time goes in v2:
time: 57.3 us; the launch traced here: 56.9 us
  Pallas kernels  50.2 us (88%)
  local copies, waits for them, and re-layouts  4.06 us (7%)
  other arithmetic  2.56 us (4%)
    pallas_call x1, Pallas kernels, node_histogram(): pl.pallas_call(hist_kernel, out_shape=jax.ShapeDtypeStruct((outputs, feat...  21.5 us
    pallas_call x1, Pallas kernels, exchange(): pl.pallas_call(exchange_kernel, out_shape=(jax.ShapeDtypeStruct(codes.sha...  21.2 us
    pallas_call x1, Pallas kernels, regroup(): pl.pallas_call(regroup_kernel, out_shape=jax.ShapeDtypeStruct((share, gro...  6.46 us
    unnamed x12, local copies, waits for them, and re-layouts  4.03 us

profile of v2, /device:TPU:8, one launch (start us, length us, event | category | flops | bytes accessed | tf_op | source)
XLA Modules:
  0.0 56.9 jit_solution(7216827020825584623)
XLA Ops:
  0.0 0.9 %convert_reduce_fusion = s32[8]{0:T(128)S(1)} fusion(s32[2048]{0:T(1024)} %param.6, s32[8]{0:T(128)} %nodes.1), kind=kLoop, calls=%fused_computation | loop fusion | flops 49144 | bytes 8256 | tf_op jit(solution)/shard_map/reduce_sum | solution.py:267
  0.9 6.5 %regroup.1.grads_ref = bf16[16,2048]{1,0:T(8,128)(2,1)} custom-call(bf16[4,16,512]{2,1,0:T(8,128)(2,1)} %bitcast.7), custom_call_target="tpu_custom_call" | custom-call | tf_op jit(solution)/shard_map/regroup/pallas_call | solution.py:50
  7.4 0.0 copy-start.1
  7.4 1.0 %copy-done.1 = s32[64,2048]{1,0:T(8,128)S(1)} copy-done((s32[64,2048]{1,0:T(8,128)S(1)}, s32[64,2048]{1,0:T(8,128)}, u32[]{:S(2)}) %copy-start.1) | copy-done | bytes 524312
  8.4 0.0 copy-start.3
  8.4 0.8 %copy-done.3 = bf16[16,2048]{1,0:T(8,128)(2,1)S(1)} copy-done((bf16[16,2048]{1,0:T(8,128)(2,1)S(1)}, bf16[16,2048]{1,0:T(8,128)(2,1)}, u32[]{:S(2)}) %copy-start.3) | copy-done | bytes 65560
  9.3 0.0 copy-start.4
  9.3 0.7 %copy-done.4 = s32[2048]{0:T(1024)S(1)} copy-done((s32[2048]{0:T(1024)S(1)}, s32[2048]{0:T(1024)}, u32[]{:S(2)}) %copy-start.4) | copy-done | bytes 8216
  10.0 0.0 copy-start.5
  10.0 0.7 %copy-done.5 = s32[8]{0:T(128)S(1)} copy-done((s32[8]{0:T(128)S(1)}, s32[8]{0:T(128)}, u32[]{:S(2)}) %copy-start.5) | copy-done | bytes 56
  10.6 1.0 %pack_windows.1 = (bf16[8,64,512]{2,1,0:T(8,128)(2,1)S(1)}, bf16[8,16,512]{2,1,0:T(8,128)(2,1)S(1)}) custom-call(s32[8]{0:T(128)S(1)} %get-tuple-element.14.starts, s32[8]{0:T(128)S(1)} %get-tuple-element.13.offsets, s32[8]{0:T(128)S(1)} %copy-done.5, s32[1,2048]{1,0:T(1,128)S(1)} %bitcast.6, s32[64,2048]{1,0:T(8,128)S(1)} %copy-done.1, ...), custom_call_target="tpu_custom_call" | custom-call | tf_op jit(solution)/shard_map/pack_windows/pallas_call | solution.py:82
  11.7 21.2 %exchange.1 = (bf16[8,64,512]{2,1,0:T(8,128)(2,1)S(1)}, bf16[8,4,16,512]{3,2,1,0:T(8,128)(2,1)S(1)}) custom-call(bf16[8,64,512]{2,1,0:T(8,128)(2,1)S(1)} %get-tuple-element.9.codes_sent, bf16[8,16,512]{2,1,0:T(8,128)(2,1)S(1)} %get-tuple-element.10.grads_sent), custom_call_target="tpu_custom_call" | custom-call | tf_op jit(solution)/shard_map/exchange/pallas_call | solution.py:153
  32.9 0.0 copy-start.2
  32.9 0.8 %copy-done.2 = bf16[8,4,16,512]{3,2,1,0:T(8,128)(2,1)} copy-done((bf16[8,4,16,512]{3,2,1,0:T(8,128)(2,1)}, bf16[8,4,16,512]{3,2,1,0:T(8,128)(2,1)S(1)}, u32[]{:S(2)}) %copy-start.2) | copy-done | bytes 524312
  33.7 0.0 copy-start
  33.7 0.1 compare_reduce_fusion
  33.8 0.1 reduce_or.9
  33.9 0.6 %convert_reduce_fusion.2 = s32[]{:T(128)} fusion(pred[32]{0:T(512)(128)(4,1)S(1)} %reduce_or.9), kind=kLoop, calls=%fused_computation.13 | loop fusion | flops 63 | bytes 36 | tf_op jit(solution)/shard_map/reduce_sum | solution.py:282
  34.6 0.1 convert_reduce_fusion.1
  34.7 0.7 %select_reduce_fusion.order = s32[32]{0:T(128)} fusion(s32[32]{0:T(128)S(1)} %convert_reduce_fusion.1, pred[32]{0:T(512)(128)(4,1)S(1)} %reduce_or.9), kind=kLoop, calls=%fused_computation.2 | loop fusion | flops 4064 | bytes 288 | tf_op jit(solution)/shard_map/reduce_sum | solution.py:281
  35.4 0.0 copy-done
  35.4 21.5 %node_histogram.1 = f32[64,8192]{1,0:T(8,128)} custom-call(s32[32]{0:T(128)} %select_reduce_fusion.order, s32[1]{0:T(128)} %bitcast.2.total, bf16[8,64,512]{2,1,0:T(8,128)(2,1)} %copy-done, bf16[8,64,512]{2,1,0:T(8,128)(2,1)} %bitcast.5), custom_call_target="tpu_custom_call" | custom-call | tf_op jit(solution)/shard_map/node_histogram/pallas_call | solution.py:241
  (2 shorter events, 0.0 us)
Async XLA Ops:
  7.4 1.0 %copy-start.1 = (s32[64,2048]{1,0:T(8,128)S(1)}, s32[64,2048]{1,0:T(8,128)}, u32[]{:S(2)}) copy-start(s32[64,2048]{1,0:T(8,128)} %codes_ref.1) | copy-start | bytes 1572868
  8.4 0.8 %copy-start.3 = (bf16[16,2048]{1,0:T(8,128)(2,1)S(1)}, bf16[16,2048]{1,0:T(8,128)(2,1)}, u32[]{:S(2)}) copy-start(bf16[16,2048]{1,0:T(8,128)(2,1)} %regroup.1.grads_ref) | copy-start | bytes 196612
  9.3 0.7 %copy-start.4 = (s32[2048]{0:T(1024)S(1)}, s32[2048]{0:T(1024)}, u32[]{:S(2)}) copy-start(s32[2048]{0:T(1024)} %param.6) | copy-start | bytes 24580
  10.0 0.7 %copy-start.5 = (s32[8]{0:T(128)S(1)}, s32[8]{0:T(128)}, u32[]{:S(2)}) copy-start(s32[8]{0:T(128)} %nodes.1) | copy-start | bytes 100
  32.9 0.8 %copy-start.2 = (bf16[8,4,16,512]{3,2,1,0:T(8,128)(2,1)}, bf16[8,4,16,512]{3,2,1,0:T(8,128)(2,1)S(1)}, u32[]{:S(2)}) copy-start(bf16[8,4,16,512]{3,2,1,0:T(8,128)(2,1)S(1)} %get-tuple-element.12) | copy-start | bytes 1572868
  33.7 1.7 %copy-start = (bf16[8,64,512]{2,1,0:T(8,128)(2,1)}, bf16[8,64,512]{2,1,0:T(8,128)(2,1)S(1)}, u32[]{:S(2)}) copy-start(bf16[8,64,512]{2,1,0:T(8,128)(2,1)S(1)} %get-tuple-element.11.codes_in) | copy-start | bytes 1572868

commit v3 on v2

--- a/solution.py
+++ b/solution.py
@@ -19,7 +19,7 @@
     lax.fori_loop(1, count, lambda d, _: (body(lax.rem(start + d, count)), 0)[1], 0)
 
 
-def regroup_kernel(grads_ref, out_ref, send, recv, own_sem):
+def regroup_kernel(grads_ref, codes_ref, out_ref, codes_out, send, recv, own_sem, codes_sem):
     groups, _, piece = grads_ref.shape
     row, feat = lax.axis_index("row"), lax.axis_index("feat")
 
@@ -35,49 +35,55 @@
     around(groups, feat, lambda f: pl.semaphore_signal(barrier, 1, device_id=(row, f), device_id_type=MESH))
     own = pltpu.make_async_copy(grads_ref.at[feat], part(feat), own_sem)
     own.start()
+    codes = pltpu.make_async_copy(codes_ref, codes_out, codes_sem)
+    codes.start()
     pl.semaphore_wait(barrier, groups - 1)
     around(groups, feat, lambda f: copy(f, feat).start())
     own.wait()
     around(groups, feat, lambda f: copy(feat, f).wait_recv())
     around(groups, feat, lambda f: copy(f, feat).wait_send())
-
-
-def regroup(grads):
+    codes.wait()
+
+
+def regroup(grads, codes):
     groups = lax.axis_size("feat")
     outputs, piece = grads.shape
     share = outputs // groups
     vectors = pl.BlockSpec(memory_space=pltpu.VMEM)
     return pl.pallas_call(
         regroup_kernel,
-        out_shape=jax.ShapeDtypeStruct((share, groups * piece), jnp.bfloat16),
-        in_specs=[vectors],
-        out_specs=vectors,
+        out_shape=(
+            jax.ShapeDtypeStruct((share, groups * piece), jnp.bfloat16),
+            jax.ShapeDtypeStruct(codes.shape, codes.dtype),
+        ),
+        in_specs=[vectors, pl.BlockSpec(memory_space=pl.ANY)],
+        out_specs=(vectors, vectors),
         scratch_shapes=[
             pltpu.SemaphoreType.DMA((groups,)),
             pltpu.SemaphoreType.DMA((groups,)),
             pltpu.SemaphoreType.DMA,
+            pltpu.SemaphoreType.DMA,
         ],
         compiler_params=pltpu.CompilerParams(collective_id=0, has_side_effects=True),
         name="regroup",
-    )(grads.reshape(groups, share, piece))
-
-
-def pack_kernel(starts, offsets, nodes, ids_ref, codes_ref, grads_ref, codes_out, grads_out):
+    )(grads.reshape(groups, share, piece), codes)
+
+
+def pack_kernel(scalars, ids_ref, codes_ref, grads_ref, codes_out, grads_out):
     slots, _, capacity = codes_out.shape
     span = capacity + LANES
     for j in range(slots):
-        window = pl.ds(pl.multiple_of(starts[j], LANES), span)
-        inside = ids_ref[:, window] == nodes[j]
+        window = pl.ds(pl.multiple_of(scalars[0, j], LANES), span)
+        inside = ids_ref[:, window] == scalars[2, j]
         part = codes_ref[:, window]
         part = jnp.where(jnp.broadcast_to(inside, part.shape), part, OUTSIDE)
-        codes_out[j] = pltpu.roll(part, offsets[j], 1)[:, :capacity].astype(jnp.float32).astype(jnp.bfloat16)
+        codes_out[j] = pltpu.roll(part, scalars[1, j], 1)[:, :capacity].astype(jnp.float32).astype(jnp.bfloat16)
         part = grads_ref[:, window].astype(jnp.float32)
-        grads_out[j] = pltpu.roll(part, offsets[j], 1)[:, :capacity].astype(jnp.bfloat16)
-
-
-def pack_windows(starts, offsets, nodes, ids, codes, grads, capacity):
-    slots = starts.shape[0]
-    scalars = pl.BlockSpec(memory_space=pltpu.SMEM)
+        grads_out[j] = pltpu.roll(part, scalars[1, j], 1)[:, :capacity].astype(jnp.bfloat16)
+
+
+def pack_windows(scalars, ids, codes, grads, capacity):
+    slots = scalars.shape[1]
     vectors = pl.BlockSpec(memory_space=pltpu.VMEM)
     return pl.pallas_call(
         pack_kernel,
@@ -85,11 +91,11 @@
             jax.ShapeDtypeStruct((slots, codes.shape[0], capacity), jnp.bfloat16),
             jax.ShapeDtypeStruct((slots, grads.shape[0], capacity), jnp.bfloat16),
         ),
-        in_specs=[scalars] * 3 + [vectors] * 3,
+        in_specs=[pl.BlockSpec(memory_space=pltpu.SMEM)] + [vectors] * 3,
         out_specs=(vectors, vectors),
         compiler_params=pltpu.CompilerParams(vmem_limit_bytes=40 << 20),
         name="pack_windows",
-    )(starts, offsets, nodes, ids, codes, grads)
+    )(scalars, ids, codes, grads)
 
 
 def exchange_kernel(
@@ -168,33 +174,41 @@
     )(codes, grads)
 
 
-def hist_kernel(order, total, codes_in, grads_in, out_ref, codes_ref, grads_ref):
-    features = out_ref.shape[1] // BINS
+def hist_kernel(counts, codes_in, grads_in, out_ref, codes_ref, lines_ref, grads_ref):
+    panels, features, capacity = codes_in.shape
     outputs = out_ref.shape[0]
-    per_panel = codes_in.shape[2] // LANES
-    most = grads_ref.shape[0] // (2 * LANES)
-
-    def gather(i, _):
-        block = order[i]
-        panel = block // per_panel
-        at = pl.multiple_of((block % per_panel) * LANES, LANES)
-        to = pl.multiple_of(i * LANES, LANES)
-        codes_ref[:, pl.ds(to, LANES)] = codes_in[panel, :, pl.ds(at, LANES)].astype(jnp.float32)
-        tile = grads_in[panel, :, pl.ds(at, LANES)].astype(jnp.float32)
-        grads_ref[pl.ds(to, LANES), :] = tile.T.astype(jnp.bfloat16)
+    span = capacity + LANES
+    step = 2 * LANES
+    most = (panels * capacity + step - 1) // step
+
+    def append(p, filled):
+        shift = filled % LANES
+        at = pl.ds(pl.multiple_of(filled // LANES * LANES, LANES), span)
+
+        def place(ref, part, fill):
+            rest = jnp.full((part.shape[0], LANES), fill, jnp.float32)
+            moved = pltpu.roll(jnp.concatenate([part.astype(jnp.float32), rest], axis=1), shift, 1)
+            lane = lax.broadcasted_iota(jnp.int32, moved.shape, 1)
+            ref[:, at] = jnp.where(lane < shift, ref[:, at], moved)
+
+        place(codes_ref, codes_in[p], float(OUTSIDE))
+        place(lines_ref, grads_in[p], 0.0)
+        return filled + counts[p]
+
+    filled = lax.fori_loop(0, panels, append, 0)
+    steps = (filled + step - 1) // step
+    tail = pl.ds(pl.multiple_of((filled + LANES - 1) // LANES * LANES, LANES), LANES)
+    codes_ref[:, tail] = jnp.full((features, LANES), OUTSIDE, jnp.float32)
+    lines_ref[:, tail] = jnp.zeros((outputs, LANES), jnp.float32)
+
+    def turn(i, _):
+        at = pl.ds(pl.multiple_of(i * step, step), step)
+        grads_ref[at, :] = lines_ref[:, at].T.astype(jnp.bfloat16)
         return 0
 
-    count = total[0]
-    lax.fori_loop(0, count, gather, 0)
-    steps = (count + 1) // 2
-
-    @pl.when(count % 2 == 1)
-    def _():
-        to = pl.multiple_of(count * LANES, LANES)
-        codes_ref[:, pl.ds(to, LANES)] = jnp.full((features, LANES), OUTSIDE, jnp.float32)
-        grads_ref[pl.ds(to, LANES), :] = jnp.zeros((LANES, outputs), jnp.bfloat16)
-
-    @pl.when(count == 0)
+    lax.fori_loop(0, steps, turn, 0)
+
+    @pl.when(filled == 0)
     def _():
         out_ref[...] = jnp.zeros_like(out_ref)
 
@@ -233,30 +247,24 @@
     lax.fori_loop(0, (steps + CHUNK - 1) // CHUNK, chunk, 0)
 
 
-def node_histogram(order, total, codes, grads):
+def node_histogram(counts, codes, grads):
     panels, features, capacity = codes.shape
     outputs = grads.shape[1]
-    blocks = panels * (capacity // LANES)
-    depth = (blocks + 1) // 2 * 2 * LANES
+    depth = panels * capacity + capacity + 2 * LANES
+    vectors = pl.BlockSpec(memory_space=pltpu.VMEM)
     return pl.pallas_call(
         hist_kernel,
         out_shape=jax.ShapeDtypeStruct((outputs, features * BINS), jnp.float32),
-        grid_spec=pltpu.PrefetchScalarGridSpec(
-            num_scalar_prefetch=2,
-            grid=(1,),
-            in_specs=[
-                pl.BlockSpec(codes.shape, lambda *_: (0, 0, 0)),
-                pl.BlockSpec(grads.shape, lambda *_: (0, 0, 0)),
-            ],
-            out_specs=pl.BlockSpec((outputs, features * BINS), lambda *_: (0, 0)),
-            scratch_shapes=[
-                pltpu.VMEM((features, depth), jnp.float32),
-                pltpu.VMEM((depth, outputs), jnp.bfloat16),
-            ],
-        ),
+        in_specs=[pl.BlockSpec(memory_space=pltpu.SMEM), vectors, vectors],
+        out_specs=vectors,
+        scratch_shapes=[
+            pltpu.VMEM((features, depth), jnp.float32),
+            pltpu.VMEM((outputs, depth), jnp.float32),
+            pltpu.VMEM((depth, outputs), jnp.bfloat16),
+        ],
         compiler_params=pltpu.CompilerParams(vmem_limit_bytes=56 << 20),
         name="node_histogram",
-    )(order, total, codes, grads)
+    )(counts, codes, grads)
 
 
 def on_device(grads, codes, node_ids, node_slot):
@@ -267,20 +275,13 @@
     row_starts = jnp.sum((node_ids[None, :] < node_slot[:, None]).astype(jnp.int32), axis=1)
     starts = jnp.minimum(row_starts // LANES * LANES, length - span)
     offsets = (span - (row_starts - starts)) % span
-    panel = regroup(grads)
-    sent = pack_windows(
-        starts, offsets, node_slot, node_ids.reshape(1, length), codes, panel, capacity
-    )
+    scalars = jnp.stack([starts, offsets, node_slot])
+    panel, codes = regroup(grads, codes)
+    sent = pack_windows(scalars, node_ids.reshape(1, length), codes, panel, capacity)
     codes_in, grads_in = exchange(*sent)
     grads_in = grads_in.reshape(grads_in.shape[0], -1, capacity)
-    blocks = codes_in.shape[0] * (capacity // LANES)
-    filled = (codes_in[:, 0, :] < BINS).reshape(blocks, LANES).any(axis=1)
-    index = jnp.arange(blocks, dtype=jnp.int32)
-    rank = jnp.sum((filled[None, :] & (index[None, :] < index[:, None])).astype(jnp.int32), axis=1)
-    hit = filled[None, :] & (rank[None, :] == index[:, None])
-    order = jnp.sum(jnp.where(hit, index[None, :], 0), axis=1)
-    total = jnp.sum(filled.astype(jnp.int32)).reshape(1)
-    return node_histogram(order, total, codes_in, grads_in)[None]
+    counts = jnp.sum((codes_in[:, 0, :] < BINS).astype(jnp.int32), axis=1)
+    return node_histogram(counts, codes_in, grads_in)[None]
 
 
 def solution(mesh):

time: 57.3 us -> 53.4 us (0.932); the launches traced: 56.9 us -> 54 us
  Pallas kernels: 50.2 us -> 48.2 us
  local copies, waits for them, and re-layouts: 4.06 us -> 3.41 us
    pallas_call x1, Pallas kernels: 21.5 us -> 19.3 us  [node_histogram(): pl.pallas_call(hist_kernel, out_shape=jax.ShapeDtypeStruct((outputs, feat...]
    reduce_sum x3 -> x1, other arithmetic: 1.46 us -> 0.73 us  [on_device(): counts = jnp.sum((codes_in[:, 0, :] < BINS).astype(jnp.int32), axis=1)]
    another operation x0 -> x1, other arithmetic: none -> 0.67 us  [on_device(): scalars = jnp.stack([starts, offsets, node_slot])]
    unnamed x12 -> x10, local copies, waits for them, and re-layouts: 4.03 us -> 3.41 us
where the time goes in v3:
time: 53.4 us; the launch traced here: 54 us
  Pallas kernels  48.2 us (90%)
  local copies, waits for them, and re-layouts  3.41 us (6%)
  other arithmetic  2.32 us (4%)
    pallas_call x1, Pallas kernels, exchange(): pl.pallas_call(exchange_kernel, out_shape=(jax.ShapeDtypeStruct(codes.sha...  21.2 us
    pallas_call x1, Pallas kernels, node_histogram(): pl.pallas_call(hist_kernel, out_shape=jax.ShapeDtypeStruct((outputs, feat...  19.3 us
    pallas_call x1, Pallas kernels, regroup(): pl.pallas_call(regroup_kernel, out_shape=(jax.ShapeDtypeStruct((share, gr...  6.65 us
    unnamed x10, local copies, waits for them, and re-layouts  3.41 us

profile of v3, /device:TPU:8, one launch (start us, length us, event | category | flops | bytes accessed | tf_op | source)
XLA Modules:
  0.0 54.0 jit_solution(17729343999199920723)
XLA Ops:
  0.0 0.9 %convert_reduce_fusion = s32[8]{0:T(128)S(1)} fusion(s32[2048]{0:T(1024)} %param.6, s32[8]{0:T(128)} %param.7), kind=kLoop, calls=%fused_computation | loop fusion | flops 49144 | bytes 8256 | tf_op jit(solution)/shard_map/reduce_sum | solution.py:275
  0.9 0.7 %pad_add_fusion.scalars = s32[3,8]{1,0:T(4,128)S(1)} fusion(s32[1,8]{1,0:T(1,128)} %bitcast.27, s32[1,8]{1,0:T(1,128)S(1)} %get-tuple-element.18, s32[1,8]{1,0:T(1,128)S(1)} %get-tuple-element.17), kind=kLoop, calls=%fused_computation.3 | loop fusion | flops 48 | bytes 192 | tf_op jit(solution)/shard_map/stack | solution.py:278
  1.6 6.7 %regroup.1 = (bf16[16,2048]{1,0:T(8,128)(2,1)}, s32[64,2048]{1,0:T(8,128)}) custom-call(bf16[4,16,512]{2,1,0:T(8,128)(2,1)} %bitcast.26, s32[64,2048]{1,0:T(8,128)} %codes_ref.1), custom_call_target="tpu_custom_call" | custom-call | tf_op jit(solution)/shard_map/regroup/pallas_call | solution.py:53
  8.2 0.0 copy-start.1
  8.3 1.0 %copy-done.1 = s32[64,2048]{1,0:T(8,128)S(1)} copy-done((s32[64,2048]{1,0:T(8,128)S(1)}, s32[64,2048]{1,0:T(8,128)}, u32[]{:S(2)}) %copy-start.1) | copy-done | bytes 524312
  9.3 0.0 copy-start.3
  9.3 0.8 %copy-done.3 = bf16[16,2048]{1,0:T(8,128)(2,1)S(1)} copy-done((bf16[16,2048]{1,0:T(8,128)(2,1)S(1)}, bf16[16,2048]{1,0:T(8,128)(2,1)}, u32[]{:S(2)}) %copy-start.3) | copy-done | bytes 65560
  10.1 0.0 copy-start.4
  10.1 0.7 %copy-done.4 = s32[2048]{0:T(1024)S(1)} copy-done((s32[2048]{0:T(1024)S(1)}, s32[2048]{0:T(1024)}, u32[]{:S(2)}) %copy-start.4) | copy-done | bytes 8216
  10.8 1.1 %pack_windows.1 = (bf16[8,64,512]{2,1,0:T(8,128)(2,1)S(1)}, bf16[8,16,512]{2,1,0:T(8,128)(2,1)S(1)}) custom-call(s32[3,8]{1,0:T(4,128)S(1)} %pad_add_fusion.scalars, s32[1,2048]{1,0:T(1,128)S(1)} %bitcast.25, s32[64,2048]{1,0:T(8,128)S(1)} %copy-done.1, bf16[16,2048]{1,0:T(8,128)(2,1)S(1)} %copy-done.3), custom_call_target="tpu_custom_call" | custom-call | tf_op jit(solution)/shard_map/pack_windows/pallas_call | solution.py:88
  11.9 21.2 %exchange.1 = (bf16[8,64,512]{2,1,0:T(8,128)(2,1)S(1)}, bf16[8,4,16,512]{3,2,1,0:T(8,128)(2,1)S(1)}) custom-call(bf16[8,64,512]{2,1,0:T(8,128)(2,1)S(1)} %get-tuple-element.13.codes_sent, bf16[8,16,512]{2,1,0:T(8,128)(2,1)S(1)} %get-tuple-element.14.grads_sent), custom_call_target="tpu_custom_call" | custom-call | tf_op jit(solution)/shard_map/exchange/pallas_call | solution.py:159
  33.1 0.0 copy-start.2
  33.1 0.8 %copy-done.2 = bf16[8,4,16,512]{3,2,1,0:T(8,128)(2,1)} copy-done((bf16[8,4,16,512]{3,2,1,0:T(8,128)(2,1)}, bf16[8,4,16,512]{3,2,1,0:T(8,128)(2,1)S(1)}, u32[]{:S(2)}) %copy-start.2) | copy-done | bytes 524312
  33.9 0.0 copy-start
  33.9 0.7 %fusion.counts = s32[8]{0:T(128)} fusion(bf16[8,64,512]{2,1,0:T(8,128)(2,1)S(1)} %get-tuple-element.15.codes_in), kind=kLoop, calls=%fused_computation.2 | loop fusion | flops 12280 | bytes 8224 | tf_op jit(solution)/shard_map/reduce_sum | solution.py:283
  34.6 0.1 copy-done
  34.7 19.3 %node_histogram.1 = f32[64,8192]{1,0:T(8,128)} custom-call(s32[8]{0:T(128)} %fusion.counts, bf16[8,64,512]{2,1,0:T(8,128)(2,1)} %copy-done, bf16[8,64,512]{2,1,0:T(8,128)(2,1)} %bitcast.24), custom_call_target="tpu_custom_call" | custom-call | tf_op jit(solution)/shard_map/node_histogram/pallas_call | solution.py:255
  (1 shorter events, 0.0 us)
Async XLA Ops:
  8.2 1.0 %copy-start.1 = (s32[64,2048]{1,0:T(8,128)S(1)}, s32[64,2048]{1,0:T(8,128)}, u32[]{:S(2)}) copy-start(s32[64,2048]{1,0:T(8,128)} %get-tuple-element.11.codes_ref) | copy-start | bytes 1572868
  9.3 0.8 %copy-start.3 = (bf16[16,2048]{1,0:T(8,128)(2,1)S(1)}, bf16[16,2048]{1,0:T(8,128)(2,1)}, u32[]{:S(2)}) copy-start(bf16[16,2048]{1,0:T(8,128)(2,1)} %get-tuple-element.12.grads_ref) | copy-start | bytes 196612
  10.1 0.7 %copy-start.4 = (s32[2048]{0:T(1024)S(1)}, s32[2048]{0:T(1024)}, u32[]{:S(2)}) copy-start(s32[2048]{0:T(1024)} %param.6) | copy-start | bytes 24580
  33.1 0.8 %copy-start.2 = (bf16[8,4,16,512]{3,2,1,0:T(8,128)(2,1)}, bf16[8,4,16,512]{3,2,1,0:T(8,128)(2,1)S(1)}, u32[]{:S(2)}) copy-start(bf16[8,4,16,512]{3,2,1,0:T(8,128)(2,1)S(1)} %get-tuple-element.16) | copy-start | bytes 1572868
  33.9 0.8 %copy-start = (bf16[8,64,512]{2,1,0:T(8,128)(2,1)}, bf16[8,64,512]{2,1,0:T(8,128)(2,1)S(1)}, u32[]{:S(2)}) copy-start(bf16[8,64,512]{2,1,0:T(8,128)(2,1)S(1)} %get-tuple-element.15.codes_in) | copy-start | bytes 1572868

commit v4 on v3

--- a/solution.py
+++ b/solution.py
@@ -64,7 +64,9 @@
             pltpu.SemaphoreType.DMA,
             pltpu.SemaphoreType.DMA,
         ],
-        compiler_params=pltpu.CompilerParams(collective_id=0, has_side_effects=True),
+        compiler_params=pltpu.CompilerParams(
+            collective_id=0, has_side_effects=True, vmem_limit_bytes=8 << 20
+        ),
         name="regroup",
     )(grads.reshape(groups, share, piece), codes)
 
@@ -93,7 +95,7 @@
         ),
         in_specs=[pl.BlockSpec(memory_space=pltpu.SMEM)] + [vectors] * 3,
         out_specs=(vectors, vectors),
-        compiler_params=pltpu.CompilerParams(vmem_limit_bytes=40 << 20),
+        compiler_params=pltpu.CompilerParams(vmem_limit_bytes=12 << 20),
         name="pack_windows",
     )(scalars, ids, codes, grads)
 
@@ -168,7 +170,7 @@
         + [pltpu.SemaphoreType.DMA((owners, groups))] * 2
         + [pltpu.SemaphoreType.DMA((2,))],
         compiler_params=pltpu.CompilerParams(
-            collective_id=1, has_side_effects=True, vmem_limit_bytes=40 << 20
+            collective_id=1, has_side_effects=True, vmem_limit_bytes=12 << 20
         ),
         name="exchange",
     )(codes, grads)
@@ -262,7 +264,7 @@
             pltpu.VMEM((outputs, depth), jnp.float32),
             pltpu.VMEM((depth, outputs), jnp.bfloat16),
         ],
-        compiler_params=pltpu.CompilerParams(vmem_limit_bytes=56 << 20),
+        compiler_params=pltpu.CompilerParams(vmem_limit_bytes=24 << 20),
         name="node_histogram",
     )(counts, codes, grads)
 

time: 53.4 us -> 50.4 us (0.944)
  the two profiles are of different devices: /device:TPU:8 before, /device:TPU:9 now
where the time goes in v4:
time: 50.4 us; the launch traced here: 49.6 us
  Pallas kernels  45.1 us (89%)
  local copies, waits for them, and re-layouts  2.57 us (5%)
  other arithmetic  1.83 us (4%)
    pallas_call x1, Pallas kernels, exchange(): pl.pallas_call(exchange_kernel, out_shape=(jax.ShapeDtypeStruct(codes.sha...  22.6 us
    pallas_call x1, Pallas kernels, node_histogram(): pl.pallas_call(hist_kernel, out_shape=jax.ShapeDtypeStruct((outputs, feat...  17.6 us
    pallas_call x1, Pallas kernels, regroup(): pl.pallas_call(regroup_kernel, out_shape=(jax.ShapeDtypeStruct((share, gr...  3.85 us
    unnamed x6, local copies, waits for them, and re-layouts  2.57 us
    pallas_call x1, Pallas kernels, pack_windows(): pl.pallas_call(pack_kernel, out_shape=(jax.ShapeDtypeStruct((slots, codes...  1.06 us

profile of v4, /device:TPU:9, one launch (start us, length us, event | category | flops | bytes accessed | tf_op | source)
XLA Modules:
  0.0 49.6 jit_solution(9243250133012855979)
XLA Ops:
  0.0 0.9 %convert_reduce_fusion = s32[8]{0:T(128)S(1)} fusion(s32[2048]{0:T(1024)} %param.6, s32[8]{0:T(128)} %param.7), kind=kLoop, calls=%fused_computation | loop fusion | flops 49144 | bytes 8256 | tf_op jit(solution)/shard_map/reduce_sum | solution.py:277
  0.9 0.7 %pad_add_fusion.scalars = s32[3,8]{1,0:T(4,128)S(1)} fusion(s32[1,8]{1,0:T(1,128)} %bitcast.27, s32[1,8]{1,0:T(1,128)S(1)} %get-tuple-element.18, s32[1,8]{1,0:T(1,128)S(1)} %get-tuple-element.17), kind=kLoop, calls=%fused_computation.3 | loop fusion | flops 48 | bytes 192 | tf_op jit(solution)/shard_map/stack | solution.py:280
  1.6 0.0 copy-start
  1.6 1.0 %copy-done = s32[64,2048]{1,0:T(8,128)S(1)} copy-done((s32[64,2048]{1,0:T(8,128)S(1)}, s32[64,2048]{1,0:T(8,128)}, u32[]{:S(2)}) %copy-start) | copy-done | bytes 524312
  2.6 0.0 copy-start.1
  2.6 0.8 %copy-done.1 = bf16[64,512]{1,0:T(8,128)(2,1)S(1)} copy-done((bf16[64,512]{1,0:T(8,128)(2,1)S(1)}, bf16[64,512]{1,0:T(8,128)(2,1)}, u32[]{:S(2)}) %copy-start.1) | copy-done | bytes 65560
  3.5 3.8 %regroup.1 = (bf16[16,2048]{1,0:T(8,128)(2,1)S(1)}, s32[64,2048]{1,0:T(8,128)S(1)}) custom-call(bf16[4,16,512]{2,1,0:T(8,128)(2,1)S(1)} %bitcast.25, s32[64,2048]{1,0:T(8,128)S(1)} %copy-done), custom_call_target="tpu_custom_call" | custom-call | tf_op jit(solution)/shard_map/regroup/pallas_call | solution.py:53
  7.3 0.0 copy-start.2
  7.3 0.7 %copy-done.2 = s32[2048]{0:T(1024)S(1)} copy-done((s32[2048]{0:T(1024)S(1)}, s32[2048]{0:T(1024)}, u32[]{:S(2)}) %copy-start.2) | copy-done | bytes 8216
  8.0 1.1 %pack_windows.1 = (bf16[8,64,512]{2,1,0:T(8,128)(2,1)S(1)}, bf16[8,16,512]{2,1,0:T(8,128)(2,1)S(1)}) custom-call(s32[3,8]{1,0:T(4,128)S(1)} %pad_add_fusion.scalars, s32[1,2048]{1,0:T(1,128)S(1)} %bitcast.26, s32[64,2048]{1,0:T(8,128)S(1)} %get-tuple-element.11.codes_ref, bf16[16,2048]{1,0:T(8,128)(2,1)S(1)} %get-tuple-element.12.grads_ref), custom_call_target="tpu_custom_call" | custom-call | tf_op jit(solution)/shard_map/pack_windows/pallas_call | solution.py:90
  9.1 22.6 %exchange.1 = (bf16[8,64,512]{2,1,0:T(8,128)(2,1)S(1)}, bf16[8,4,16,512]{3,2,1,0:T(8,128)(2,1)S(1)}) custom-call(bf16[8,64,512]{2,1,0:T(8,128)(2,1)S(1)} %get-tuple-element.13.codes_sent, bf16[8,16,512]{2,1,0:T(8,128)(2,1)S(1)} %get-tuple-element.14.grads_sent), custom_call_target="tpu_custom_call" | custom-call | tf_op jit(solution)/shard_map/exchange/pallas_call | solution.py:161
  31.7 0.2 fusion.counts
  32.0 17.6 %node_histogram.1 = f32[64,8192]{1,0:T(8,128)} custom-call(s32[8]{0:T(128)S(1)} %fusion.counts, bf16[8,64,512]{2,1,0:T(8,128)(2,1)S(1)} %get-tuple-element.15.codes_in, bf16[8,64,512]{2,1,0:T(8,128)(2,1)S(1)} %bitcast.24), custom_call_target="tpu_custom_call" | custom-call | tf_op jit(solution)/shard_map/node_histogram/pallas_call | solution.py:257
  (1 shorter events, 0.0 us)
Async XLA Ops:
  1.6 1.0 %copy-start = (s32[64,2048]{1,0:T(8,128)S(1)}, s32[64,2048]{1,0:T(8,128)}, u32[]{:S(2)}) copy-start(s32[64,2048]{1,0:T(8,128)} %codes_ref.1) | copy-start | bytes 1572868
  2.6 0.8 %copy-start.1 = (bf16[64,512]{1,0:T(8,128)(2,1)S(1)}, bf16[64,512]{1,0:T(8,128)(2,1)}, u32[]{:S(2)}) copy-start(bf16[64,512]{1,0:T(8,128)(2,1)} %param.4) | copy-start | bytes 196612
  7.3 0.7 %copy-start.2 = (s32[2048]{0:T(1024)S(1)}, s32[2048]{0:T(1024)}, u32[]{:S(2)}) copy-start(s32[2048]{0:T(1024)} %param.6) | copy-start | bytes 24580
